TPU v7x, 512 devices: a whole 4x4x16 slice. The times are simulated.
512 devices in a mesh: outer: 8 (over x, y_lo), inner: 64 (over z, y_hi, core).
Axes of the slice: x: 4, y: 4 (y_hi: 2, y_lo: 2; y = y_hi * 2 + y_lo), z: 16, core: 2. Of those that a mesh axis runs over, the one named last changes fastest.
Arguments:
- queries: bfloat16 [16384, 2048], P('inner'), may hold values from -128 to 128
- mem_keys: bfloat16 [8192, 2048], P(('outer', 'inner')), may hold values from -4.5 to 4.5
- mem_values: bfloat16 [8192, 2048], P(('outer', 'inner')), may hold values from -6 to 6
Outputs:
- attended: bfloat16 [16384, 2048], P('inner')
- log_total: float32 [16384, 16], P('inner')
All inputs are finite; a program needn't handle non-finite values.
Results may differ from a plain program's by a relative error of at most 0.014.
Values may be sent and summed in bfloat16 or wider, within the bound.
No kernel may reach another device: no remote copies, remote signals or barrier semaphores. Data moves between devices by JAX's collectives and lax.ppermute only.
A program may use at most 64 MiB of HBM per device.

v0:
```python
import math
import jax
import jax.numpy as jnp
from jax import lax
from jax.sharding import PartitionSpec as P

HEADS = 16
HEAD_DIM = 128


def on_device(queries, mem_keys, mem_values):
    row_count = queries.shape[0]
    columns = queries.shape[1]
    scale = 1.0 / math.sqrt(HEAD_DIM)
    query_heads = queries.reshape(row_count, HEADS, HEAD_DIM)
    initial = (
        jnp.full((row_count, HEADS), -jnp.inf, jnp.float32),
        jnp.zeros((row_count, HEADS), jnp.float32),
        jnp.zeros((row_count, HEADS, HEAD_DIM), jnp.float32),
    )
    key_piece = lax.all_gather(mem_keys, "inner", axis=0, tiled=True)
    value_piece = lax.all_gather(mem_values, "inner", axis=0, tiled=True)
    entries = key_piece.shape[0]
    block = math.gcd(entries, 256)
    key_blocks = key_piece.reshape(entries // block, block, HEADS, HEAD_DIM)
    value_blocks = value_piece.reshape(entries // block, block, HEADS, HEAD_DIM)

    def one_block(running, blocks):
        running_top, running_total, running_out = running
        key_block, value_block = blocks
        scores = (
            jnp.einsum("thd,khd->thk", query_heads, key_block, preferred_element_type=jnp.float32)
            * scale
        )
        new_top = jnp.maximum(running_top, jnp.max(scores, axis=-1))
        fading = jnp.exp(running_top - new_top)
        raw = jnp.exp(scores - new_top[..., None])
        new_total = running_total * fading + jnp.sum(raw, axis=-1)
        product = jnp.einsum(
            "thk,khd->thd",
            raw.astype(jnp.bfloat16),
            value_block,
            preferred_element_type=jnp.float32,
        )
        new_out = running_out * fading[..., None] + product
        return ((new_top, new_total, new_out), None)

    result, unused = lax.scan(one_block, initial, (key_blocks, value_blocks))
    group_peak, group_total, group_out = result
    peak = lax.pmax(group_peak, "outer")
    factor = jnp.exp(group_peak - peak)
    weighted = (group_out * factor[..., None]).reshape(row_count, columns)
    total = lax.psum(group_total * factor, "outer")
    log_total = peak + jnp.log(total)
    summed = lax.psum(weighted.astype(jnp.bfloat16), "outer").astype(jnp.float32)
    attended = (
        (summed.reshape(row_count, HEADS, HEAD_DIM) / total[..., None])
        .astype(jnp.bfloat16)
        .reshape(row_count, columns)
    )
    return (attended, log_total)


def solution(mesh):
    in_specs = (P("inner", None), P(("outer", "inner"), None), P(("outer", "inner"), None))
    out_specs = (P("inner", None), P("inner", None))
    return jax.shard_map(
        on_device, mesh=mesh, in_specs=in_specs, out_specs=out_specs, check_vma=False
    )
```

profile of v0, /device:TPU:32, one launch (start us, length us, event | category | flops | bytes accessed | tf_op | source)
XLA Modules:
  0.0 486.1 jit_solution(9600157572781027679)
XLA Ops:
  7.2 0.0 all-gather.3.cloned.1.call-start
  7.2 0.7 all-gather.3.cloned.1.call-update
  7.9 0.0 all-gather.5.cloned.1.call-start
  7.9 0.7 all-gather.5.cloned.1.call-update
  8.6 0.0 all-reduce.2.cloned.1.call-start
  8.7 1.5 copy.9
  10.2 1.3 copy.11
  11.5 154.5 %all-gather.3.cloned.1.call-done = bf16[1024,2048]{1,0:T(8,128)(2,1)} async-done(((bf16[16,2048]{1,0:T(8,128)(2,1)}), bf16[1024,2048]{1,0:T(8,128)(2,1)}) %all-gather.3.cloned.1.call-update) | async-done | bytes 4194320 | tf_op jit(solution)/shard_map/all_gather | solution.py:21
  166.0 5.5 %copy.19 = bf16[128,8,16,128]{3,2,1,0:T(8,128)(2,1)} copy(bf16[128,8,16,128]{3,1,2,0:T(8,128)(2,1)} %bitcast.54) | data formatting | bytes 8388608
  171.6 142.9 %all-gather.5.cloned.1.call-done = bf16[1024,2048]{1,0:T(8,128)(2,1)} async-done(((bf16[16,2048]{1,0:T(8,128)(2,1)}), bf16[1024,2048]{1,0:T(8,128)(2,1)}) %all-gather.5.cloned.1.call-update) | async-done | bytes 4194320 | tf_op jit(solution)/shard_map/all_gather | solution.py:22
  314.4 5.6 %copy.20 = bf16[128,8,16,128]{3,2,1,0:T(8,128)(2,1)} copy(bf16[128,8,16,128]{3,1,2,0:T(8,128)(2,1)} %bitcast.55) | data formatting | bytes 8388608
  320.0 33.2 %while.15 = (s32[]{:T(128)}, f32[256,16]{0,1:T(8,128)S(1)}, f32[256,16]{0,1:T(8,128)S(1)}, f32[256,16,128]{0,2,1:T(8,128)}, bf16[4,256,16,128]{3,2,1,0:T(8,128)(...) while((s32[]{:T(128)}, f32[256,16]{0,1:T(8,128)S(1)}, ...), condition=%wide.region_3.4_spmd.clone, body=%wide.region_0.3_spmd.clone.sunk | while | flops 546852864 | bytes 43253932 | solution.py:48
  320.0 1.9 constant_dynamic-slice_fusion.3
  321.9 0.8 copy.30
  322.7 0.0 copy-start
  322.7 2.1 bitcast_reduce_fusion.2
  324.8 0.7 fusion.24
  325.6 0.0 copy-done
  325.6 1.4 bitcast_add_fusion.2
  326.9 0.0 copy-start.1
  327.0 1.3 copy-done.1
  328.3 1.9 constant_dynamic-slice_fusion.3
  330.2 0.8 copy.30
  331.0 0.0 copy-start
  331.0 2.1 bitcast_reduce_fusion.2
  333.1 0.7 fusion.24
  333.8 0.0 copy-done
  333.9 1.4 bitcast_add_fusion.2
  335.2 0.0 copy-start.1
  335.3 1.3 copy-done.1
  336.6 1.9 constant_dynamic-slice_fusion.3
  338.5 0.8 copy.30
  339.3 0.0 copy-start
  339.3 2.1 bitcast_reduce_fusion.2
  341.4 0.7 fusion.24
  342.1 0.0 copy-done
  342.2 1.4 bitcast_add_fusion.2
  343.5 0.0 copy-start.1
  343.6 1.3 copy-done.1
  344.9 1.9 constant_dynamic-slice_fusion.3
  346.8 0.8 copy.30
  347.6 0.0 copy-start
  347.6 2.1 bitcast_reduce_fusion.2
  349.7 0.7 fusion.24
  350.4 0.0 copy-done
  350.5 1.4 bitcast_add_fusion.2
  351.8 0.0 copy-start.1
  351.9 1.3 copy-done.1
  353.2 33.2 %pmax.7 = f32[256,16]{0,1:T(8,128)S(1)} all-reduce(f32[256,16]{0,1:T(8,128)S(1)} %get-tuple-element.42), channel_id=1, replica_groups=mesh['outer'=8,'inner'=64] {'outer'}, use_global_device_ids=true, to_apply=%region_4.5 | all-reduce | flops 4096 | bytes 32768 | tf_op jit(solution)/shard_map/pmax | solution.py:50
  386.4 1.8 multiply_convert_fusion
  388.2 1.4 copy.16
  389.6 0.0 all-reduce.2.cloned.1.call-update
  389.6 31.2 %psum.15 = f32[256,16]{0,1:T(8,128)S(1)} all-reduce(f32[256,16]{0,1:T(8,128)S(1)} %get-tuple-element.91), channel_id=1, replica_groups=mesh['outer'=8,'inner'=64] {'outer'}, use_global_device_ids=true, to_apply=%region_6.7 | all-reduce | flops 4096 | bytes 32768 | tf_op jit(solution)/shard_map/psum | solution.py:53
  420.8 0.1 copy.14
  420.9 0.6 log_add_fusion
  421.6 54.3 %all-reduce.2.cloned.1.call-done = bf16[256,2048]{1,0:T(8,128)(2,1)} async-done(((bf16[256,2048]{1,0:T(8,128)(2,1)}), bf16[256,2048]{1,0:T(8,128)(2,1)}) %all-reduce.2.cloned.1.call-update) | async-done | bytes 1048592 | tf_op jit(solution)/shard_map/psum | solution.py:55
  475.9 0.6 div.11
  476.5 3.1 fusion.13
  (16 shorter events, 0.1 us)
Async XLA Ops:
  7.2 158.9 %all-gather.3.cloned.1.call-start = ((), (), s32[]{:S(2)}) async-start(), calls=%async_computation | async-start | bytes 4259840 | tf_op jit(solution)/shard_map/all_gather | solution.py:21
  7.9 306.5 %all-gather.5.cloned.1.call-start = ((), (), s32[]{:S(2)}) async-start(), calls=%async_computation.1 | async-start | bytes 4259840 | tf_op jit(solution)/shard_map/all_gather | solution.py:22
  8.6 467.2 %all-reduce.2.cloned.1.call-start = ((), (), s32[]{:S(2)}) async-start(), calls=%async_computation.2 | async-start | bytes 2097152 | tf_op jit(solution)/shard_map/psum | solution.py:55
  322.7 2.9 copy-start
  326.9 1.3 copy-start.1
  331.0 2.9 copy-start
  335.2 1.3 copy-start.1
  339.3 2.9 copy-start
  343.5 1.3 copy-start.1
  347.6 2.9 copy-start
  351.8 1.3 copy-start.1
Sparse Core Ops, SparseCore 0:
  11.3 154.7 all-gather.2
  169.3 145.0 all-gather.4
  389.7 86.0 all-reduce.1
where the time goes:
time: 487 us; the launch traced here: 486 us
  waiting for transfers between devices  353 us (72%)
  blocking collectives  64.4 us (13%)
  local copies, waits for them, and re-layouts  32.1 us (7%)
  matrix products  13.9 us (3%)
  between operations  13.8 us (3%)
  other arithmetic  8.47 us (2%)
    all_gather x1, waiting for transfers between devices, on_device(): key_piece = lax.all_gather(mem_keys, 'inner', axis=0, tiled=True)  154 us
    all_gather x1, waiting for transfers between devices, on_device(): value_piece = lax.all_gather(mem_values, 'inner', axis=0, tiled=True)  143 us
    psum x1, waiting for transfers between devices, on_device(): lax.psum(weighted.astype(jnp.bfloat16), 'outer').astype(jnp.float32)  54.3 us
    pmax x1, blocking collectives, on_device(): peak = lax.pmax(group_peak, 'outer')  33.2 us
    psum x1, blocking collectives, on_device(): total = lax.psum(group_total * factor, 'outer')  31.2 us
    unnamed x4, local copies, waits for them, and re-layouts  13.9 us
    dynamic_slice x8, local copies, waits for them, and re-layouts, on_device(): result, unused = lax.scan(one_block, initial, (key_blocks, value_blocks))  10.8 us
  transfers between devices with their start and end apart: 3, of which 3 were waited for; matrix products, arithmetic and copies ran while one was open for 2% of the time, Pallas kernels for 0%

commit v1 on v0

--- a/solution.py
+++ b/solution.py
@@ -9,6 +9,18 @@
 
 
 def on_device(queries, mem_keys, mem_values):
+
+    def begin_cycles(field_in):
+        return jnp.concatenate(
+            jax.lax.all_to_all(
+                jnp.stack(tuple((field_in for _ in range(jax.lax.axis_size("inner"))))),
+                "inner",
+                split_axis=0,
+                concat_axis=0,
+            ),
+            axis=0,
+        )
+
     row_count = queries.shape[0]
     columns = queries.shape[1]
     scale = 1.0 / math.sqrt(HEAD_DIM)
@@ -19,7 +31,7 @@
         jnp.zeros((row_count, HEADS, HEAD_DIM), jnp.float32),
     )
     key_piece = lax.all_gather(mem_keys, "inner", axis=0, tiled=True)
-    value_piece = lax.all_gather(mem_values, "inner", axis=0, tiled=True)
+    value_piece = begin_cycles(mem_values)
     entries = key_piece.shape[0]
     block = math.gcd(entries, 256)
     key_blocks = key_piece.reshape(entries // block, block, HEADS, HEAD_DIM)

time: 487 us -> 413 us (0.85)
  waiting for transfers between devices: 353 us -> 258 us
  starting transfers between devices: 0.11 us -> 18.8 us
    all_gather x1 -> x0, waiting for transfers between devices: 143 us -> none  [on_device(): value_piece = lax.all_gather(mem_values, 'inner', axis=0, tiled=True)]
    all_gather x1, waiting for transfers between devices: 154 us -> 197 us  [on_device(): key_piece = lax.all_gather(mem_keys, 'inner', axis=0, tiled=True)]
    all_to_all x0 -> x1, starting transfers between devices: none -> 18.7 us  [begin_cycles(): jax.lax.all_to_all(jnp.stack(tuple((field_in for _ in range(jax.lax.axis_...]
    psum x1, waiting for transfers between devices: 54.3 us -> 59.9 us  [on_device(): lax.psum(weighted.astype(jnp.bfloat16), 'outer').astype(jnp.float32)]
    unnamed x4 -> x6, local copies, waits for them, and re-layouts: 13.9 us -> 12.9 us
where the time goes in v1:
time: 413 us; the launch traced here: 412 us
  waiting for transfers between devices  258 us (62%)
  blocking collectives  63.9 us (15%)
  local copies, waits for them, and re-layouts  34.5 us (8%)
  starting transfers between devices  18.8 us (5%)
  between operations  14.1 us (3%)
  matrix products  13.9 us (3%)
  other arithmetic  8.47 us (2%)
    all_gather x1, waiting for transfers between devices, on_device(): key_piece = lax.all_gather(mem_keys, 'inner', axis=0, tiled=True)  197 us
    psum x1, waiting for transfers between devices, on_device(): lax.psum(weighted.astype(jnp.bfloat16), 'outer').astype(jnp.float32)  59.9 us
    pmax x1, blocking collectives, on_device(): peak = lax.pmax(group_peak, 'outer')  33.2 us
    psum x1, blocking collectives, on_device(): total = lax.psum(group_total * factor, 'outer')  30.7 us
    all_to_all x1, starting transfers between devices, begin_cycles(): jax.lax.all_to_all(jnp.stack(tuple((field_in for _ in range(jax.lax.axis_...  18.7 us
    unnamed x6, local copies, waits for them, and re-layouts  12.9 us
    dynamic_slice x8, local copies, waits for them, and re-layouts, on_device(): result, unused = lax.scan(one_block, initial, (key_blocks, value_blocks))  10.8 us
    dot_general x4, matrix products, one_block(): jnp.einsum('thd,khd->thk', query_heads, key_block, preferred_element_type...  8.38 us
  transfers between devices with their start and end apart: 3, of which 3 were waited for; matrix products, arithmetic and copies ran while one was open for 2% of the time, Pallas kernels for 0%

profile of v1, /device:TPU:32, one launch (start us, length us, event | category | flops | bytes accessed | tf_op | source)
XLA Modules:
  0.0 412.0 jit_solution(16932424578292645740)
XLA Ops:
  7.2 3.3 stack.2
  10.5 0.0 copy-start.2
  10.5 18.7 %all-to-all-start = ((bf16[64,16,2048]{2,1,0:T(8,128)(2,1)}), bf16[64,16,2048]{2,1,0:T(8,128)(2,1)}, u32[]{:S(2)}, u32[]{:S(2)}) async-start(bf16[64,16,2048]{2,1,0:T(8,128)(2,1)} %stack.2), calls=%async_computation | async-start | bytes 8388608 | tf_op jit(solution)/shard_map/all_to_all | solution.py:15
  29.2 0.0 all-gather.2.cloned.1.call-start
  29.3 0.7 all-gather.2.cloned.1.call-update
  29.9 0.0 all-reduce.2.cloned.1.call-start
  30.0 0.0 copy-done.2
  30.0 0.5 copy.9
  30.6 1.3 copy.11
  31.9 196.8 %all-gather.2.cloned.1.call-done = bf16[1024,2048]{1,0:T(8,128)(2,1)} async-done(((bf16[16,2048]{1,0:T(8,128)(2,1)}), bf16[1024,2048]{1,0:T(8,128)(2,1)}) %all-gather.2.cloned.1.call-update) | async-done | bytes 4194320 | tf_op jit(solution)/shard_map/all_gather | solution.py:33
  228.7 5.5 %copy.19 = bf16[128,8,16,128]{3,2,1,0:T(8,128)(2,1)} copy(bf16[128,8,16,128]{3,1,2,0:T(8,128)(2,1)} %bitcast.55) | data formatting | bytes 8388608
  234.2 0.7 all-to-all-done
  234.9 5.6 %copy.20 = bf16[128,8,16,128]{3,2,1,0:T(8,128)(2,1)} copy(bf16[128,8,16,128]{3,1,2,0:T(8,128)(2,1)} %bitcast.10) | data formatting | bytes 8388608
  240.5 33.2 %while.15 = (s32[]{:T(128)}, f32[256,16]{0,1:T(8,128)S(1)}, f32[256,16]{0,1:T(8,128)S(1)}, f32[256,16,128]{0,2,1:T(8,128)}, bf16[4,256,16,128]{3,2,1,0:T(8,128)(...) while((s32[]{:T(128)}, f32[256,16]{0,1:T(8,128)S(1)}, ...), condition=%wide.region_3.4_spmd.clone, body=%wide.region_0.3_spmd.clone.sunk | while | flops 546852864 | bytes 43253932 | solution.py:60
  240.5 1.9 constant_dynamic-slice_fusion.3
  242.4 0.8 copy.30
  243.2 0.0 copy-start
  243.2 2.1 bitcast_reduce_fusion.2
  245.3 0.7 fusion.24
  246.0 0.0 copy-done
  246.1 1.4 bitcast_add_fusion.2
  247.4 0.0 copy-start.1
  247.4 1.3 copy-done.1
  248.8 1.9 constant_dynamic-slice_fusion.3
  250.7 0.8 copy.30
  251.5 0.0 copy-start
  251.5 2.1 bitcast_reduce_fusion.2
  253.6 0.7 fusion.24
  254.3 0.0 copy-done
  254.3 1.4 bitcast_add_fusion.2
  255.7 0.0 copy-start.1
  255.7 1.3 copy-done.1
  257.1 1.9 constant_dynamic-slice_fusion.3
  259.0 0.8 copy.30
  259.8 0.0 copy-start
  259.8 2.1 bitcast_reduce_fusion.2
  261.9 0.7 fusion.24
  262.6 0.0 copy-done
  262.6 1.4 bitcast_add_fusion.2
  264.0 0.0 copy-start.1
  264.0 1.3 copy-done.1
  265.4 1.9 constant_dynamic-slice_fusion.3
  267.3 0.8 copy.30
  268.1 0.0 copy-start
  268.1 2.1 bitcast_reduce_fusion.2
  270.2 0.7 fusion.24
  270.9 0.0 copy-done
  270.9 1.4 bitcast_add_fusion.2
  272.3 0.0 copy-start.1
  272.3 1.3 copy-done.1
  273.7 33.2 %pmax.7 = f32[256,16]{0,1:T(8,128)S(1)} all-reduce(f32[256,16]{0,1:T(8,128)S(1)} %get-tuple-element.42), channel_id=1, replica_groups=mesh['outer'=8,'inner'=64] {'outer'}, use_global_device_ids=true, to_apply=%region_4.5 | all-reduce | flops 4096 | bytes 32768 | tf_op jit(solution)/shard_map/pmax | solution.py:62
  306.8 1.8 multiply_convert_fusion
  308.6 1.4 copy.16
  310.1 0.0 all-reduce.2.cloned.1.call-update
  310.1 30.7 %psum.15 = f32[256,16]{0,1:T(8,128)S(1)} all-reduce(f32[256,16]{0,1:T(8,128)S(1)} %get-tuple-element.91), channel_id=1, replica_groups=mesh['outer'=8,'inner'=64] {'outer'}, use_global_device_ids=true, to_apply=%region_6.7 | all-reduce | flops 4096 | bytes 32768 | tf_op jit(solution)/shard_map/psum | solution.py:65
  340.8 0.1 copy.14
  340.9 0.6 log_add_fusion
  341.5 59.9 %all-reduce.2.cloned.1.call-done = bf16[256,2048]{1,0:T(8,128)(2,1)} async-done(((bf16[256,2048]{1,0:T(8,128)(2,1)}), bf16[256,2048]{1,0:T(8,128)(2,1)}) %all-reduce.2.cloned.1.call-update) | async-done | bytes 1048592 | tf_op jit(solution)/shard_map/psum | solution.py:67
  401.5 0.6 div.11
  402.1 3.1 fusion.13
  (16 shorter events, 0.1 us)
Async XLA Ops:
  10.5 19.5 %copy-start.2 = (bf16[256,2048]{1,0:T(8,128)(2,1)S(1)}, bf16[256,2048]{1,0:T(8,128)(2,1)}, u32[]{:S(2)}) copy-start(bf16[256,2048]{1,0:T(8,128)(2,1)} %param.5) | copy-start | bytes 3145732
  10.5 224.4 %all-to-all-start = ((bf16[64,16,2048]{2,1,0:T(8,128)(2,1)}), bf16[64,16,2048]{2,1,0:T(8,128)(2,1)}, u32[]{:S(2)}, u32[]{:S(2)}) async-start(bf16[64,16,2048]{2,1,0:T(8,128)(2,1)} %stack.2), calls=%async_computation | async-start | bytes 8388608 | tf_op jit(solution)/shard_map/all_to_all | solution.py:15
  29.2 199.4 %all-gather.2.cloned.1.call-start = ((), (), s32[]{:S(2)}) async-start(), calls=%async_computation.1 | async-start | bytes 4259840 | tf_op jit(solution)/shard_map/all_gather | solution.py:33
  29.9 371.5 %all-reduce.2.cloned.1.call-start = ((), (), s32[]{:S(2)}) async-start(), calls=%async_computation.2 | async-start | bytes 2097152 | tf_op jit(solution)/shard_map/psum | solution.py:67
  243.2 2.9 copy-start
  247.4 1.3 copy-start.1
  251.5 2.9 copy-start
  255.7 1.3 copy-start.1
  259.8 2.9 copy-start
  264.0 1.3 copy-start.1
  268.1 2.9 copy-start
  272.3 1.3 copy-start.1
Sparse Core Ops, SparseCore 0:
  33.3 195.2 all-gather.1
  310.2 91.1 all-reduce.1
